TPU v7x, 512 devices: a whole 4x8x8 slice. The times are simulated.
512 devices in a mesh: ctx: 32 (over y, x), head: 16 (over z, core).
Axes of the slice: x: 4, y: 8, z: 8, core: 2. Of those that a mesh axis runs over, the one named last changes fastest.
Arguments:
- activations: bfloat16 [8192, 16384], P('ctx'), may hold values from -6 to 6
- w_query: bfloat16 [16384, 2048], P('ctx', 'head'), may hold values from -0.046875 to 0.046875
- w_keyval: bfloat16 [16384, 256], P('ctx', 'head'), may hold values from -0.046875 to 0.046875
- f_query: bfloat16 [16, 128, 128], P('head'), may hold values from -1 to 1
- f_key: bfloat16 [128, 128], replicated, may hold values from -1 to 1
- w_out: bfloat16 [2048, 16384], P('ctx', 'head'), may hold values from -0.75 to 0.75
Outputs:
- sublayer_out: bfloat16 [8192, 16384], P('ctx', 'head')
All inputs are finite; a program needn't handle non-finite values.
Results may differ from a plain program's by a relative error of at most 0.0086.
Values may be sent and summed in bfloat16 or wider, within the bound.
A program may use at most 64 MiB of HBM per device.

v0:
```python
import math
import jax
import jax.numpy as jnp
from jax import lax
from jax.sharding import PartitionSpec as P

WINDOW = 64


def from_behind(array, axis, by):
    size = lax.axis_size(axis)
    pairs = [(i, i + by) for i in range(size) if 0 <= i + by < size]
    return lax.ppermute(array, axis, pairs)


def prefix(array, axis, combine, identity):
    size, mine = (lax.axis_size(axis), lax.axis_index(axis))
    everything = jax.tree.map(
        lambda part, kind: lax.all_gather(part.astype(kind), axis),
        array,
        jax.tree.map(lambda a: jnp.bfloat16 if a.dtype == jnp.float32 else a.dtype, array),
    )
    start = jax.tree.map(
        lambda part, zero: jnp.broadcast_to(jnp.asarray(zero, part.dtype), part.shape),
        array,
        identity,
    )

    def step(k, before):
        reached = k < mine
        new = combine(
            before, jax.tree.map(lambda part, own: part[k].astype(own.dtype), everything, array)
        )
        return jax.tree.map(lambda a, b: jnp.where(reached, a, b), new, before)

    return lax.fori_loop(0, size, step, start)


def normalized(logits):
    rising = jnp.exp(logits)
    falling = jnp.exp(-logits)
    rising = rising / jnp.sum(rising, axis=-1, keepdims=True)
    falling = falling / jnp.sum(falling, axis=-1, keepdims=True)
    return jnp.concatenate([rising, falling], axis=-1).astype(jnp.bfloat16)


def state_of(features, values):
    matrix = jnp.einsum("nf,nc->fc", features, values, preferred_element_type=jnp.float32)
    totals = jnp.sum(features.astype(jnp.float32), axis=0)
    return (matrix, totals)


def add_states(earlier, later):
    return (earlier[0] + later[0], earlier[1] + later[1])


def per_device(activations, w_query, w_keyval, f_query, f_key, w_out):
    length = activations.shape[0]
    head_width = f_key.shape[0]
    local_heads = f_query.shape[0]
    columns = activations
    query_sum = jnp.dot(
        columns,
        lax.all_gather(w_query, "ctx", axis=0, tiled=True),
        preferred_element_type=jnp.float32,
    )
    pair_sum = jnp.dot(
        columns,
        lax.all_gather(w_keyval, "ctx", axis=0, tiled=True),
        preferred_element_type=jnp.float32,
    )
    queries = query_sum.astype(jnp.bfloat16)
    keyval = lax.all_gather(pair_sum.astype(jnp.bfloat16), "head", axis=1, tiled=True)
    border = from_behind(keyval[length - WINDOW :], "ctx", 1)
    extended = jnp.concatenate([border, keyval], axis=0)
    ext_keys = extended[:, :head_width]
    ext_vals = extended[:, head_width:]
    first_pos = lax.axis_index("ctx") * length - WINDOW
    present = first_pos + jnp.arange(length + WINDOW) >= 0
    ext_feats = normalized(jnp.dot(ext_keys, f_key, preferred_element_type=jnp.float32))
    ext_feats = jnp.where(present[:, None], ext_feats, jnp.zeros_like(ext_feats))
    contribution = state_of(ext_feats[:length], ext_vals[:length])
    identity = (
        jnp.zeros((2 * head_width, head_width), jnp.float32),
        jnp.zeros((2 * head_width,), jnp.float32),
    )
    matrix, totals = prefix(contribution, "ctx", add_states, identity)
    query_heads = queries.reshape(length, local_heads, head_width)
    query_feats = normalized(
        jnp.einsum("thc,hcf->htf", query_heads, f_query, preferred_element_type=jnp.float32)
    )
    offsets = jnp.arange(length)[:, None] + WINDOW - jnp.arange(length + WINDOW)[None, :]
    inside = (offsets >= 0) & (offsets < WINDOW) & present[None, :]
    beyond = (offsets >= WINDOW) & present[None, :]
    scale = 1.0 / math.sqrt(head_width)
    scores = (
        jnp.einsum("thc,kc->htk", query_heads, ext_keys, preferred_element_type=jnp.float32) * scale
    )
    near_w = jnp.where(inside[None], jnp.exp(scores), 0.0)
    far_w = jnp.where(
        beyond[None],
        jnp.einsum("htf,kf->htk", query_feats, ext_feats, preferred_element_type=jnp.float32),
        0.0,
    )
    weights = near_w + far_w
    feats_wide = query_feats.astype(jnp.float32)
    numerator = jnp.einsum(
        "htk,kc->htc", weights, ext_vals.astype(jnp.float32), precision=lax.Precision.HIGHEST
    )
    numerator = numerator + jnp.einsum(
        "htf,fc->htc", feats_wide, matrix, precision=lax.Precision.HIGHEST
    )
    denominator = jnp.sum(weights, axis=-1) + jnp.einsum(
        "htf,f->ht", feats_wide, totals, precision=lax.Precision.HIGHEST
    )
    attn_heads = (numerator / denominator[..., None]).astype(jnp.bfloat16)
    attn_rows = jnp.transpose(attn_heads, (1, 0, 2)).reshape(length, local_heads * head_width)
    all_heads = lax.all_gather(attn_rows, "head", axis=1, tiled=True)
    columns = all_heads
    projected = jnp.dot(
        columns,
        lax.all_gather(w_out, "ctx", axis=0, tiled=True),
        preferred_element_type=jnp.float32,
    )
    return projected.astype(jnp.bfloat16)


def solution(mesh):
    in_specs = (
        P("ctx", None),
        P("ctx", "head"),
        P("ctx", "head"),
        P("head", None, None),
        P(),
        P("ctx", "head"),
    )
    out_specs = P("ctx", "head")
    return jax.shard_map(
        per_device, mesh=mesh, in_specs=in_specs, out_specs=out_specs, check_vma=False
    )
```

profile of v0, /device:TPU:1, one launch (start us, length us, event | category | flops | bytes accessed | tf_op | source)
XLA Modules:
  0.0 402.4 jit_solution(3140013990136511824)
XLA Ops:
  6.5 39.9 %all_gather.27 = bf16[16384,16]{0,1:T(8,128)(2,1)S(1)} all-gather(bf16[512,16]{0,1:T(8,128)(2,1)} %param.10), channel_id=1, replica_groups=mesh['ctx'=32,'head'=16] {'ctx'}, dimensions={0}, use_global_device_ids=true | all-gather | bytes 540672 | tf_op jit(solution)/shard_map/all_gather | solution.py:69
  46.5 5.6 %convolution_convert_fusion.3 = bf16[256,16]{0,1:T(8,128)(2,1)S(1)} fusion(bf16[256,16384]{1,0:T(8,128)(2,1)} %param.8, bf16[16384,16]{0,1:T(8,128)(2,1)S(1)} %all_gather.27), kind=kOutput, calls=%fused_computation.16 | convolution fusion | flops 134221824 | bytes 8921088 | tf_op jit(solution)/shard_map/dot_general | solution.py:67
  52.1 35.5 %all_gather.28 = bf16[256,256]{0,1:T(8,128)(2,1)S(1)} all-gather(bf16[256,16]{0,1:T(8,128)(2,1)S(1)} %convolution_convert_fusion.3), channel_id=1, replica_groups=mesh['ctx'=32,'head'=16] {'head'}, dimensions={1}, use_global_device_ids=true | all-gather | bytes 139264 | tf_op jit(solution)/shard_map/all_gather | solution.py:73
  87.7 2.4 collective-permute-start
  90.1 1.3 collective-permute-done
  94.7 35.3 %all-gather.2 = bf16[32,1,256]{2,1,0:T(2,128)(2,1)S(1)} all-gather(bf16[1,1,256]{2,1,0:T(2,128)(2,1)S(1)} %reshape.161), channel_id=3, replica_groups=mesh['ctx'=32,'head'=16] {'ctx'}, dimensions={0}, use_global_device_ids=true | all-gather | bytes 16896 | tf_op jit(solution)/shard_map/all_gather | solution.py:19
  130.0 41.1 %all-gather.14.cloned.1.call-done = bf16[8192,128]{1,0:T(8,128)(2,1)} async-done(((bf16[256,128]{1,0:T(8,128)(2,1)}), bf16[8192,128]{1,0:T(8,128)(2,1)}) %all-gather.14.cloned.1.call-update) | async-done | bytes 2097168 | tf_op jit(solution)/shard_map/all_gather | solution.py:19
  171.1 30.8 %while.16 = (s32[]{:T(128)}, f32[256,128]{1,0:T(8,128)S(1)}, f32[256]{0:T(256)S(1)}, s32[]{:T(128)}, bf16[32,256,128]{2,1,0:T(8,128)(2,1)}, /*index=5*/bf16[32,256]{1,0:T(8,128)(2,1)S(1)}, s32[]{:T(128)}, s32[]{:T(128)}) while((s32[]{:T(128)}, f32[256,128]{1,0:T(8,128)S(1)}, f32[256]{0:T(256)S(1)}, s32[]{:T(128)}, ...), condition=%wide.region_6.7_spmd.clone, body=%wide.region_5.6_spmd.clone.sunk | while | flops 132100 | bytes 332403 | solution.py:36
  172.1 0.9 add_select_fusion.4
  173.1 0.9 add_select_fusion.4
  174.0 0.9 add_select_fusion.4
  175.0 0.9 add_select_fusion.4
  175.9 0.9 add_select_fusion.4
  176.9 0.9 add_select_fusion.4
  177.9 0.9 add_select_fusion.4
  178.8 0.9 add_select_fusion.4
  179.8 0.9 add_select_fusion.4
  180.8 0.9 add_select_fusion.4
  181.7 0.9 add_select_fusion.4
  186.6 0.9 add_select_fusion.4
  189.4 0.9 add_select_fusion.4
  190.4 0.9 add_select_fusion.4
  191.4 0.9 add_select_fusion.4
  192.3 0.9 add_select_fusion.4
  195.2 0.9 add_select_fusion.4
  198.1 0.9 add_select_fusion.4
  202.0 58.0 %all-gather.8.cloned.1.call-done = bf16[16384,128]{1,0:T(8,128)(2,1)} async-done(((bf16[512,128]{1,0:T(8,128)(2,1)}), bf16[16384,128]{1,0:T(8,128)(2,1)}) %all-gather.8.cloned.1.call-update) | async-done | bytes 4194320 | tf_op jit(solution)/shard_map/all_gather | solution.py:64
  260.0 6.9 %convolution_convert_fusion.2 = bf16[256,128]{1,0:T(8,128)(2,1)S(1)} fusion(bf16[256,16384]{1,0:T(8,128)(2,1)} %param.8, bf16[16384,128]{1,0:T(8,128)(2,1)} %all-gather.8.cloned.1.call-done), kind=kOutput, calls=%fused_computation.15 | convolution fusion | flops 1073774592 | bytes 12648448 | tf_op jit(solution)/shard_map/dot_general | solution.py:62
  268.3 1.2 fusion.6
  269.5 78.3 %all-gather.12.cloned.1.call-done = bf16[2048,1024]{1,0:T(8,128)(2,1)} async-done(((bf16[64,1024]{1,0:T(8,128)(2,1)}), bf16[2048,1024]{1,0:T(8,128)(2,1)}) %all-gather.12.cloned.1.call-update) | async-done | bytes 4194320 | tf_op jit(solution)/shard_map/all_gather | solution.py:122
  347.8 43.5 %all-gather.10.cloned.1.call-done = bf16[256,2048]{1,0:T(8,128)(2,1)} async-done(((bf16[256,128]{1,0:T(8,128)(2,1)}), bf16[256,2048]{1,0:T(8,128)(2,1)}) %all-gather.10.cloned.1.call-update) | async-done | bytes 1048592 | tf_op jit(solution)/shard_map/all_gather | solution.py:118
  391.3 4.6 %convolution_convert_fusion = bf16[256,1024]{1,0:T(8,128)(2,1)} fusion(bf16[256,2048]{1,0:T(8,128)(2,1)} %all-gather.10.cloned.1.call-done, bf16[2048,1024]{1,0:T(8,128)(2,1)} %all-gather.12.cloned.1.call-done), kind=kOutput, calls=%fused_computation.3 | convolution fusion | flops 1074003968 | bytes 5767168 | tf_op jit(solution)/shard_map/dot_general | solution.py:120
  (109 shorter events, 18.2 us)
Async XLA Ops:
  6.5 84.9 %copy-start = (bf16[128,128]{1,0:T(8,128)(2,1)S(1)}, bf16[128,128]{1,0:T(8,128)(2,1)}, u32[]{:S(2)}) copy-start(bf16[128,128]{1,0:T(8,128)(2,1)} %param.12) | copy-start | bytes 98308
  6.5 164.6 %all-gather.14.cloned.1.call-start = ((), (), s32[]{:S(2)}) async-start(), calls=%async_computation.3 | async-start | bytes 2162688 | tf_op jit(solution)/shard_map/all_gather | solution.py:19
  87.7 3.7 collective-permute-start
  93.1 166.9 %all-gather.8.cloned.1.call-start = ((), (), s32[]{:S(2)}) async-start(), calls=%async_computation | async-start | bytes 4325376 | tf_op jit(solution)/shard_map/all_gather | solution.py:64
  93.9 253.9 %all-gather.12.cloned.1.call-start = ((), (), s32[]{:S(2)}) async-start(), calls=%async_computation.2 | async-start | bytes 4325376 | tf_op jit(solution)/shard_map/all_gather | solution.py:122
  94.6 296.7 %all-gather.10.cloned.1.call-start = ((), (), s32[]{:S(2)}) async-start(), calls=%async_computation.1 | async-start | bytes 1114112 | tf_op jit(solution)/shard_map/all_gather | solution.py:118
  202.0 64.9 %copy-start.1 = (bf16[1,128,128]{2,1,0:T(8,128)(2,1)S(1)}, bf16[1,128,128]{2,1,0:T(8,128)(2,1)}, u32[]{:S(2)}) copy-start(bf16[1,128,128]{2,1,0:T(8,128)(2,1)} %param.11) | copy-start | bytes 98308
Sparse Core Ops, SparseCore 0:
  93.2 77.8 all-gather.13
  174.3 85.6 all-gather.7
  263.1 84.6 all-gather.11
  349.7 41.5 all-gather.9
where the time goes:
time: 404 us; the launch traced here: 402 us
  waiting for transfers between devices  224 us (55%)
  blocking collectives  111 us (27%)
  other arithmetic  30.2 us (7%)
  matrix products  21 us (5%)
  between operations  13.3 us (3%)
    all_gather x1, waiting for transfers between devices, per_device(): lax.all_gather(w_out, 'ctx', axis=0, tiled=True)  78.3 us
    all_gather x1, waiting for transfers between devices, per_device(): lax.all_gather(w_query, 'ctx', axis=0, tiled=True)  58 us
    all_gather x1, waiting for transfers between devices, per_device(): all_heads = lax.all_gather(attn_rows, 'head', axis=1, tiled=True)  43.5 us
    all_gather x1, waiting for transfers between devices, prefix(): lax.all_gather(part.astype(kind), axis)  41.1 us
    all_gather x1, blocking collectives, per_device(): lax.all_gather(w_keyval, 'ctx', axis=0, tiled=True)  39.9 us
    all_gather x1, blocking collectives, per_device(): lax.all_gather(pair_sum.astype(jnp.bfloat16), 'head', axis=1, tiled=True)  35.5 us
    all_gather x1, blocking collectives, prefix(): lax.all_gather(part.astype(kind), axis)  35.3 us
    select_n x64, other arithmetic, step(): return jax.tree.map(lambda a, b: jnp.where(reached, a, b), new, before)  29.3 us
  transfers between devices with their start and end apart: 5, of which 5 were waited for; matrix products, arithmetic and copies ran while one was open for 10% of the time, Pallas kernels for 0%

commit v1 on v0

--- a/solution.py
+++ b/solution.py
@@ -115,7 +115,25 @@
     )
     attn_heads = (numerator / denominator[..., None]).astype(jnp.bfloat16)
     attn_rows = jnp.transpose(attn_heads, (1, 0, 2)).reshape(length, local_heads * head_width)
-    all_heads = lax.all_gather(attn_rows, "head", axis=1, tiled=True)
+    length_2, index, rows = (lax.axis_size("head"), lax.axis_index("head"), attn_rows.shape[1])
+    ahead = [(i_2, (i_2 + 1) % length_2) for i_2 in range(length_2)]
+    left = [(i_2, (i_2 - 1) % length_2) for i_2 in range(length_2)]
+    all_heads = jnp.zeros(
+        (*attn_rows.shape[:1], length_2 * rows, *attn_rows.shape[1 + 1 :]), attn_rows.dtype
+    )
+    all_heads = lax.dynamic_update_slice_in_dim(all_heads, attn_rows, index * rows, axis=1)
+    from_left = from_right = attn_rows
+    halfway = length_2 // 2
+    for step_2 in range(1, halfway + 1):
+        from_left = lax.ppermute(from_left, "head", ahead)
+        all_heads = lax.dynamic_update_slice_in_dim(
+            all_heads, from_left, (index - step_2) % length_2 * rows, axis=1
+        )
+        if step_2 < length_2 - halfway:
+            from_right = lax.ppermute(from_right, "head", left)
+            all_heads = lax.dynamic_update_slice_in_dim(
+                all_heads, from_right, (index + step_2) % length_2 * rows, axis=1
+            )
     columns = all_heads
     projected = jnp.dot(
         columns,

time: 404 us -> 362 us (0.90)
  waiting for transfers between devices: 224 us -> 154 us
  starting transfers between devices: 2.53 us -> 28.9 us
    all_gather x1 -> x0, waiting for transfers between devices: 43.5 us -> none  [per_device(): all_heads = lax.all_gather(attn_rows, 'head', axis=1, tiled=True)]
    all_gather x1, waiting for transfers between devices: 78.3 us -> 40.5 us  [per_device(): lax.all_gather(w_out, 'ctx', axis=0, tiled=True)]
    ppermute x0 -> x15, starting transfers between devices: none -> 26.4 us  [the longest x7 14.9 us: per_device(): from_right = lax.ppermute(from_right, 'head', left)]
    ppermute x0 -> x15, waiting for transfers between devices: none -> 11.4 us  [the longest x8 8.4 us: per_device(): from_left = lax.ppermute(from_left, 'head', ahead)]
  transfers between devices with their start and end apart: 5 -> 19, of which waited for: 5 -> 16; matrix products, arithmetic and copies ran while one was open for 10% -> 11% of each run, Pallas kernels for 0% -> 0%
where the time goes in v1:
time: 362 us; the launch traced here: 359 us
  waiting for transfers between devices  154 us (43%)
  blocking collectives  111 us (31%)
  other arithmetic  30.1 us (8%)
  starting transfers between devices  28.9 us (8%)
  matrix products  20.1 us (6%)
  between operations  13.4 us (4%)
    all_gather x1, waiting for transfers between devices, per_device(): lax.all_gather(w_query, 'ctx', axis=0, tiled=True)  58 us
    all_gather x1, waiting for transfers between devices, prefix(): lax.all_gather(part.astype(kind), axis)  41.1 us
    all_gather x1, waiting for transfers between devices, per_device(): lax.all_gather(w_out, 'ctx', axis=0, tiled=True)  40.5 us
    all_gather x1, blocking collectives, per_device(): lax.all_gather(w_keyval, 'ctx', axis=0, tiled=True)  39.9 us
    all_gather x1, blocking collectives, per_device(): lax.all_gather(pair_sum.astype(jnp.bfloat16), 'head', axis=1, tiled=True)  35.5 us
    all_gather x1, blocking collectives, prefix(): lax.all_gather(part.astype(kind), axis)  35.3 us
    select_n x64, other arithmetic, step(): return jax.tree.map(lambda a, b: jnp.where(reached, a, b), new, before)  29.3 us
    ppermute x7, starting transfers between devices, per_device(): from_right = lax.ppermute(from_right, 'head', left)  14.9 us
  transfers between devices with their start and end apart: 19, of which 16 were waited for; matrix products, arithmetic and copies ran while one was open for 11% of the time, Pallas kernels for 0%

profile of v1, /device:TPU:1, one launch (start us, length us, event | category | flops | bytes accessed | tf_op | source)
XLA Modules:
  0.0 358.6 jit_solution(5445764282447821433)
XLA Ops:
  6.5 39.9 %all_gather.24 = bf16[16384,16]{0,1:T(8,128)(2,1)S(1)} all-gather(bf16[512,16]{0,1:T(8,128)(2,1)} %param.10), channel_id=1, replica_groups=mesh['ctx'=32,'head'=16] {'ctx'}, dimensions={0}, use_global_device_ids=true | all-gather | bytes 540672 | tf_op jit(solution)/shard_map/all_gather | solution.py:69
  46.5 5.6 %convolution_convert_fusion.3 = bf16[256,16]{0,1:T(8,128)(2,1)S(1)} fusion(bf16[256,16384]{1,0:T(8,128)(2,1)} %param.8, bf16[16384,16]{0,1:T(8,128)(2,1)S(1)} %all_gather.24), kind=kOutput, calls=%fused_computation.16 | convolution fusion | flops 134221824 | bytes 8921088 | tf_op jit(solution)/shard_map/dot_general | solution.py:67
  52.1 35.5 %all_gather.25 = bf16[256,256]{0,1:T(8,128)(2,1)S(1)} all-gather(bf16[256,16]{0,1:T(8,128)(2,1)S(1)} %convolution_convert_fusion.3), channel_id=1, replica_groups=mesh['ctx'=32,'head'=16] {'head'}, dimensions={1}, use_global_device_ids=true | all-gather | bytes 139264 | tf_op jit(solution)/shard_map/all_gather | solution.py:73
  87.7 2.4 collective-permute-start
  90.1 1.3 collective-permute-done
  94.7 35.3 %all-gather.2 = bf16[32,1,256]{2,1,0:T(2,128)(2,1)S(1)} all-gather(bf16[1,1,256]{2,1,0:T(2,128)(2,1)S(1)} %reshape.161), channel_id=3, replica_groups=mesh['ctx'=32,'head'=16] {'ctx'}, dimensions={0}, use_global_device_ids=true | all-gather | bytes 16896 | tf_op jit(solution)/shard_map/all_gather | solution.py:19
  130.0 41.1 %all-gather.11.cloned.1.call-done = bf16[8192,128]{1,0:T(8,128)(2,1)} async-done(((bf16[256,128]{1,0:T(8,128)(2,1)}), bf16[8192,128]{1,0:T(8,128)(2,1)}) %all-gather.11.cloned.1.call-update) | async-done | bytes 2097168 | tf_op jit(solution)/shard_map/all_gather | solution.py:19
  171.1 30.8 %while.16 = (s32[]{:T(128)}, f32[256,128]{1,0:T(8,128)S(1)}, f32[256]{0:T(256)S(1)}, s32[]{:T(128)}, bf16[32,256,128]{2,1,0:T(8,128)(2,1)}, /*index=5*/bf16[32,256]{1,0:T(8,128)(2,1)S(1)}, s32[]{:T(128)}, s32[]{:T(128)}) while((s32[]{:T(128)}, f32[256,128]{1,0:T(8,128)S(1)}, f32[256]{0:T(256)S(1)}, s32[]{:T(128)}, ...), condition=%wide.region_6.7_spmd.clone, body=%wide.region_5.6_spmd.clone.sunk | while | flops 132100 | bytes 332403 | solution.py:36
  172.1 0.9 add_select_fusion.4
  173.1 0.9 add_select_fusion.4
  174.0 0.9 add_select_fusion.4
  175.0 0.9 add_select_fusion.4
  175.9 0.9 add_select_fusion.4
  189.4 0.9 add_select_fusion.4
  190.4 0.9 add_select_fusion.4
  191.4 0.9 add_select_fusion.4
  199.1 0.9 add_select_fusion.4
  201.9 58.0 %all-gather.7.cloned.1.call-done = bf16[16384,128]{1,0:T(8,128)(2,1)} async-done(((bf16[512,128]{1,0:T(8,128)(2,1)}), bf16[16384,128]{1,0:T(8,128)(2,1)}) %all-gather.7.cloned.1.call-update) | async-done | bytes 4194320 | tf_op jit(solution)/shard_map/all_gather | solution.py:64
  260.0 6.9 %convolution_convert_fusion.2 = bf16[256,128]{1,0:T(8,128)(2,1)S(1)} fusion(bf16[256,16384]{1,0:T(8,128)(2,1)} %param.8, bf16[16384,128]{1,0:T(8,128)(2,1)} %all-gather.7.cloned.1.call-done), kind=kOutput, calls=%fused_computation.15 | convolution fusion | flops 1073774592 | bytes 12648448 | tf_op jit(solution)/shard_map/dot_general | solution.py:62
  269.0 4.4 %collective-permute-start.1 = (bf16[256,128]{1,0:T(8,128)(2,1)S(1)}, bf16[256,128]{1,0:T(8,128)(2,1)S(1)}, u32[]{:S(2)}, u32[]{:S(2)}) collective-permute-start(bf16[256,128]{1,0:T(8,128)(2,1)S(1)} %get-tuple-element.163), channel_id=1, source_target_pairs={{0,1},{1,2},{2,3},{3,4},{4,5},{5,6},{6,7},{7,8},{8,9},{9,10},{10,1... | collective-permute-start | bytes 196616 | tf_op jit(solution)/shard_map/ppermute | solution.py:128
  273.5 1.3 collective-permute-done.1
  274.8 2.4 collective-permute-start.3
  277.2 1.3 collective-permute-done.3
  278.5 2.4 collective-permute-start.5
  282.8 1.8 collective-permute-start.7
  284.8 2.1 collective-permute-start.8
  288.6 3.5 collective-permute-start.10
  293.0 4.4 %collective-permute-start.12 = (bf16[256,128]{1,0:T(8,128)(2,1)S(1)}, bf16[256,128]{1,0:T(8,128)(2,1)S(1)}, u32[]{:S(2)}, u32[]{:S(2)}) collective-permute-start(bf16[256,128]{1,0:T(8,128)(2,1)S(1)} %collective-permute-done.10), channel_id=1, source_target_pairs={{0,15},{1,0},{2,1},{3,2},{4,3},{5,4},{6,5},{7,6},{8,7},{9,8},{10,9... | collective-permute-start | bytes 196616 | tf_op jit(solution)/shard_map/ppermute | solution.py:133
  298.3 4.0 %collective-permute-start.14 = (bf16[256,128]{1,0:T(8,128)(2,1)S(1)}, bf16[256,128]{1,0:T(8,128)(2,1)S(1)}, u32[]{:S(2)}, u32[]{:S(2)}) collective-permute-start(bf16[256,128]{1,0:T(8,128)(2,1)S(1)} %collective-permute-done.12), channel_id=1, source_target_pairs={{0,15},{1,0},{2,1},{3,2},{4,3},{5,4},{6,5},{7,6},{8,7},{9,8},{10,9... | collective-permute-start | bytes 196616 | tf_op jit(solution)/shard_map/ppermute | solution.py:133
  303.3 4.0 %collective-permute-done.15 = bf16[256,128]{1,0:T(8,128)(2,1)S(1)} collective-permute-done((bf16[256,128]{1,0:T(8,128)(2,1)S(1)}, bf16[256,128]{1,0:T(8,128)(2,1)S(1)}, u32[]{:S(2)}, u32[]{:S(2)}) %collective-permute-start.15) | collective-permute-done | bytes 65568 | tf_op jit(solution)/shard_map/ppermute | solution.py:128
  307.3 40.5 %all-gather.9.cloned.1.call-done = bf16[2048,1024]{1,0:T(8,128)(2,1)} async-done(((bf16[64,1024]{1,0:T(8,128)(2,1)}), bf16[2048,1024]{1,0:T(8,128)(2,1)}) %all-gather.9.cloned.1.call-update) | async-done | bytes 4194320 | tf_op jit(solution)/shard_map/all_gather | solution.py:140
  347.8 4.2 %convolution_convert_fusion = bf16[256,1024]{1,0:T(8,128)(2,1)} fusion(bf16[256,2048]{1,0:T(8,128)(2,1)S(1)} %constant_dynamic-update-slice_fusion, bf16[2048,1024]{1,0:T(8,128)(2,1)} %all-gather.9.cloned.1.call-done), kind=kOutput, calls=%fused_computation.3 | convolution fusion | flops 1074003968 | bytes 5767168 | tf_op jit(solution)/shard_map/dot_general | solution.py:138
  (152 shorter events, 33.6 us)
Async XLA Ops:
  6.5 84.9 %copy-start = (bf16[128,128]{1,0:T(8,128)(2,1)S(1)}, bf16[128,128]{1,0:T(8,128)(2,1)}, u32[]{:S(2)}) copy-start(bf16[128,128]{1,0:T(8,128)(2,1)} %param.12) | copy-start | bytes 98308
  6.5 164.6 %all-gather.11.cloned.1.call-start = ((), (), s32[]{:S(2)}) async-start(), calls=%async_computation.2 | async-start | bytes 2162688 | tf_op jit(solution)/shard_map/all_gather | solution.py:19
  87.7 3.7 %collective-permute-start = (bf16[64,256]{0,1:T(8,128)(2,1)S(1)}, bf16[64,256]{0,1:T(8,128)(2,1)S(1)}, u32[]{:S(2)}, u32[]{:S(2)}) collective-permute-start(bf16[64,256]{0,1:T(8,128)(2,1)S(1)} %slice.21), channel_id=1, source_target_pairs={{0,16},{16,32},{32,48},{48,64},{64,80},{80,96},{96,112},{112,128},... | collective-permute-start | bytes 98312 | tf_op jit(solution)/shard_map/ppermute | solution.py:13
  93.1 166.9 %all-gather.7.cloned.1.call-start = ((), (), s32[]{:S(2)}) async-start(), calls=%async_computation | async-start | bytes 4325376 | tf_op jit(solution)/shard_map/all_gather | solution.py:64
  93.9 253.9 %all-gather.9.cloned.1.call-start = ((), (), s32[]{:S(2)}) async-start(), calls=%async_computation.1 | async-start | bytes 4325376 | tf_op jit(solution)/shard_map/all_gather | solution.py:140
  201.9 64.9 %copy-start.1 = (bf16[1,128,128]{2,1,0:T(8,128)(2,1)S(1)}, bf16[1,128,128]{2,1,0:T(8,128)(2,1)}, u32[]{:S(2)}) copy-start(bf16[1,128,128]{2,1,0:T(8,128)(2,1)} %param.11) | copy-start | bytes 98308
  269.0 5.8 %collective-permute-start.1 = (bf16[256,128]{1,0:T(8,128)(2,1)S(1)}, bf16[256,128]{1,0:T(8,128)(2,1)S(1)}, u32[]{:S(2)}, u32[]{:S(2)}) collective-permute-start(bf16[256,128]{1,0:T(8,128)(2,1)S(1)} %get-tuple-element.163), channel_id=1, source_target_pairs={{0,1},{1,2},{2,3},{3,4},{4,5},{5,6},{6,7},{7,8},{8,9},{9,10},{10,1... | collective-permute-start | bytes 196616 | tf_op jit(solution)/shard_map/ppermute | solution.py:128
  273.5 3.7 %collective-permute-start.2 = (bf16[256,128]{1,0:T(8,128)(2,1)S(1)}, bf16[256,128]{1,0:T(8,128)(2,1)S(1)}, u32[]{:S(2)}, u32[]{:S(2)}) collective-permute-start(bf16[256,128]{1,0:T(8,128)(2,1)S(1)} %get-tuple-element.163), channel_id=1, source_target_pairs={{0,15},{1,0},{2,1},{3,2},{4,3},{5,4},{6,5},{7,6},{8,7},{9,8},{10,9... | collective-permute-start | bytes 196616 | tf_op jit(solution)/shard_map/ppermute | solution.py:133
  274.8 3.7 %collective-permute-start.3 = (bf16[256,128]{1,0:T(8,128)(2,1)S(1)}, bf16[256,128]{1,0:T(8,128)(2,1)S(1)}, u32[]{:S(2)}, u32[]{:S(2)}) collective-permute-start(bf16[256,128]{1,0:T(8,128)(2,1)S(1)} %collective-permute-done.1), channel_id=1, source_target_pairs={{0,1},{1,2},{2,3},{3,4},{4,5},{5,6},{6,7},{7,8},{8,9},{9,10},{10,1... | collective-permute-start | bytes 196616 | tf_op jit(solution)/shard_map/ppermute | solution.py:128
  277.2 4.0 %collective-permute-start.4 = (bf16[256,128]{1,0:T(8,128)(2,1)S(1)}, bf16[256,128]{1,0:T(8,128)(2,1)S(1)}, u32[]{:S(2)}, u32[]{:S(2)}) collective-permute-start(bf16[256,128]{1,0:T(8,128)(2,1)S(1)} %collective-permute-done.2), channel_id=1, source_target_pairs={{0,15},{1,0},{2,1},{3,2},{4,3},{5,4},{6,5},{7,6},{8,7},{9,8},{10,9... | collective-permute-start | bytes 196616 | tf_op jit(solution)/shard_map/ppermute | solution.py:133
  278.5 4.3 %collective-permute-start.5 = (bf16[256,128]{1,0:T(8,128)(2,1)S(1)}, bf16[256,128]{1,0:T(8,128)(2,1)S(1)}, u32[]{:S(2)}, u32[]{:S(2)}) collective-permute-start(bf16[256,128]{1,0:T(8,128)(2,1)S(1)} %collective-permute-done.3), channel_id=1, source_target_pairs={{0,1},{1,2},{2,3},{3,4},{4,5},{5,6},{6,7},{7,8},{8,9},{9,10},{10,1... | collective-permute-start | bytes 196616 | tf_op jit(solution)/shard_map/ppermute | solution.py:128
  281.1 3.7 %collective-permute-start.6 = (bf16[256,128]{1,0:T(8,128)(2,1)S(1)}, bf16[256,128]{1,0:T(8,128)(2,1)S(1)}, u32[]{:S(2)}, u32[]{:S(2)}) collective-permute-start(bf16[256,128]{1,0:T(8,128)(2,1)S(1)} %collective-permute-done.4), channel_id=1, source_target_pairs={{0,15},{1,0},{2,1},{3,2},{4,3},{5,4},{6,5},{7,6},{8,7},{9,8},{10,9... | collective-permute-start | bytes 196616 | tf_op jit(solution)/shard_map/ppermute | solution.py:133
  282.8 4.9 %collective-permute-start.7 = (bf16[256,128]{1,0:T(8,128)(2,1)S(1)}, bf16[256,128]{1,0:T(8,128)(2,1)S(1)}, u32[]{:S(2)}, u32[]{:S(2)}) collective-permute-start(bf16[256,128]{1,0:T(8,128)(2,1)S(1)} %collective-permute-done.5), channel_id=1, source_target_pairs={{0,1},{1,2},{2,3},{3,4},{4,5},{5,6},{6,7},{7,8},{8,9},{9,10},{10,1... | collective-permute-start | bytes 196616 | tf_op jit(solution)/shard_map/ppermute | solution.py:128
  284.8 3.8 %collective-permute-start.8 = (bf16[256,128]{1,0:T(8,128)(2,1)S(1)}, bf16[256,128]{1,0:T(8,128)(2,1)S(1)}, u32[]{:S(2)}, u32[]{:S(2)}) collective-permute-start(bf16[256,128]{1,0:T(8,128)(2,1)S(1)} %collective-permute-done.6), channel_id=1, source_target_pairs={{0,15},{1,0},{2,1},{3,2},{4,3},{5,4},{6,5},{7,6},{8,7},{9,8},{10,9... | collective-permute-start | bytes 196616 | tf_op jit(solution)/shard_map/ppermute | solution.py:133
  287.7 4.9 %collective-permute-start.9 = (bf16[256,128]{1,0:T(8,128)(2,1)S(1)}, bf16[256,128]{1,0:T(8,128)(2,1)S(1)}, u32[]{:S(2)}, u32[]{:S(2)}) collective-permute-start(bf16[256,128]{1,0:T(8,128)(2,1)S(1)} %collective-permute-done.7), channel_id=1, source_target_pairs={{0,1},{1,2},{2,3},{3,4},{4,5},{5,6},{6,7},{7,8},{8,9},{9,10},{10,1... | collective-permute-start | bytes 196616 | tf_op jit(solution)/shard_map/ppermute | solution.py:128
  288.6 4.4 %collective-permute-start.10 = (bf16[256,128]{1,0:T(8,128)(2,1)S(1)}, bf16[256,128]{1,0:T(8,128)(2,1)S(1)}, u32[]{:S(2)}, u32[]{:S(2)}) collective-permute-start(bf16[256,128]{1,0:T(8,128)(2,1)S(1)} %collective-permute-done.8), channel_id=1, source_target_pairs={{0,15},{1,0},{2,1},{3,2},{4,3},{5,4},{6,5},{7,6},{8,7},{9,8},{10,9... | collective-permute-start | bytes 196616 | tf_op jit(solution)/shard_map/ppermute | solution.py:133
  292.6 4.9 %collective-permute-start.11 = (bf16[256,128]{1,0:T(8,128)(2,1)S(1)}, bf16[256,128]{1,0:T(8,128)(2,1)S(1)}, u32[]{:S(2)}, u32[]{:S(2)}) collective-permute-start(bf16[256,128]{1,0:T(8,128)(2,1)S(1)} %collective-permute-done.9), channel_id=1, source_target_pairs={{0,1},{1,2},{2,3},{3,4},{4,5},{5,6},{6,7},{7,8},{8,9},{9,10},{10,1... | collective-permute-start | bytes 196616 | tf_op jit(solution)/shard_map/ppermute | solution.py:128
  293.0 5.3 %collective-permute-start.12 = (bf16[256,128]{1,0:T(8,128)(2,1)S(1)}, bf16[256,128]{1,0:T(8,128)(2,1)S(1)}, u32[]{:S(2)}, u32[]{:S(2)}) collective-permute-start(bf16[256,128]{1,0:T(8,128)(2,1)S(1)} %collective-permute-done.10), channel_id=1, source_target_pairs={{0,15},{1,0},{2,1},{3,2},{4,3},{5,4},{6,5},{7,6},{8,7},{9,8},{10,9... | collective-permute-start | bytes 196616 | tf_op jit(solution)/shard_map/ppermute | solution.py:133
  297.5 4.9 %collective-permute-start.13 = (bf16[256,128]{1,0:T(8,128)(2,1)S(1)}, bf16[256,128]{1,0:T(8,128)(2,1)S(1)}, u32[]{:S(2)}, u32[]{:S(2)}) collective-permute-start(bf16[256,128]{1,0:T(8,128)(2,1)S(1)} %collective-permute-done.11), channel_id=1, source_target_pairs={{0,1},{1,2},{2,3},{3,4},{4,5},{5,6},{6,7},{7,8},{8,9},{9,10},{10,1... | collective-permute-start | bytes 196616 | tf_op jit(solution)/shard_map/ppermute | solution.py:128
  298.3 4.9 %collective-permute-start.14 = (bf16[256,128]{1,0:T(8,128)(2,1)S(1)}, bf16[256,128]{1,0:T(8,128)(2,1)S(1)}, u32[]{:S(2)}, u32[]{:S(2)}) collective-permute-start(bf16[256,128]{1,0:T(8,128)(2,1)S(1)} %collective-permute-done.12), channel_id=1, source_target_pairs={{0,15},{1,0},{2,1},{3,2},{4,3},{5,4},{6,5},{7,6},{8,7},{9,8},{10,9... | collective-permute-start | bytes 196616 | tf_op jit(solution)/shard_map/ppermute | solution.py:133
  302.4 4.9 %collective-permute-start.15 = (bf16[256,128]{1,0:T(8,128)(2,1)S(1)}, bf16[256,128]{1,0:T(8,128)(2,1)S(1)}, u32[]{:S(2)}, u32[]{:S(2)}) collective-permute-start(bf16[256,128]{1,0:T(8,128)(2,1)S(1)} %collective-permute-done.13), channel_id=1, source_target_pairs={{0,1},{1,2},{2,3},{3,4},{4,5},{5,6},{6,7},{7,8},{8,9},{9,10},{10,1... | collective-permute-start | bytes 196616 | tf_op jit(solution)/shard_map/ppermute | solution.py:128
Sparse Core Ops, SparseCore 0:
  93.2 77.8 all-gather.10
  174.3 85.6 all-gather.6
  263.1 84.6 all-gather.8
